TPU v7x, 256 devices: a whole 4x4x8 slice. The times are simulated.
256 devices in a mesh: feat: 16 (over z, y_lo), cand: 16 (over x, y_hi, core).
Axes of the slice: x: 4, y: 4 (y_hi: 2, y_lo: 2; y = y_hi * 2 + y_lo), z: 8, core: 2. Of those that a mesh axis runs over, the one named last changes fastest.
Arguments:
- cand_grads: bfloat16 [1024, 1048576], P('cand', 'feat'), may hold values from -30 to 30
- val_grads: bfloat16 [256, 1048576], P('cand', 'feat'), may hold values from -30 to 30
- second_moment: float32 [1048576], P('feat'), may hold values from 0.0005 to 1.5
- slot_blocks: int32 [8, 128], replicated, may hold values from 0 to 127, as said below
- slot_seeds: int32 [8, 128], replicated, may hold values from 0 to 1073741823
Outputs:
- scores: float32 [1024, 64], P('cand', 'feat')
Inputs may be any that keep to these rules, and one draw needn't show every extreme that they name: `slot_blocks`: each row is a permutation of the input blocks; with L = 128 / (devices of feat), G = (devices of feat) / 8, and o_k = k * G for even k and (k - 1) * G + 1 for odd k, slot k of output block b reads an input block whose index divided by L equals (b / L + o_k) modulo the devices of feat (divisions rounded down).
All inputs are finite; a program needn't handle non-finite values.
Results may differ from a plain program's by a relative error of at most 0.0003.
Values sent between devices are 32-bit elements; how exact they have to be, the bound alone decides.
No kernel may reach another device: no remote copies, remote signals or barrier semaphores. Data moves between devices by JAX's collectives and lax.ppermute only.
A program may use at most 64 MiB of HBM per device.

v0:
```python
import math
import jax
import jax.numpy as jnp
from jax import lax
from jax.sharding import PartitionSpec as P

PB = 8192
FEATS = 8192
FB = 64
SLOTS = 8
VPT = 4


def block_signs(seed_val, height, breadth):
    across = lax.broadcasted_iota(jnp.int32, (height, breadth), 0)
    column = lax.broadcasted_iota(jnp.int32, (height, breadth), 1)
    mixed = seed_val ^ across * jnp.int32(73856093) ^ column * jnp.int32(19349663)
    for repeat in range(2):
        mixed = mixed ^ lax.shift_right_logical(mixed, jnp.int32(16))
        mixed = mixed * jnp.int32(73244475)
    mixed = mixed ^ lax.shift_right_logical(mixed, jnp.int32(16))
    return (2 * (mixed & 1) - 1).astype(jnp.float32)


def signs_for(seed_val):
    return block_signs(seed_val, PB, FB)


def squares(features):
    return jnp.sum(features * features, axis=(0, 2))


def body(cand_grads, val_grads, second_moment, slot_blocks, slot_seeds):
    local_blocks = second_moment.shape[0] // PB
    first_block = lax.axis_index("feat") * local_blocks
    groups = FEATS // 128
    per_group = 128 // FB
    factor = 1.0 / math.sqrt(SLOTS * PB)
    ncand = cand_grads.shape[0]
    wide = cand_grads.astype(jnp.float32)
    adam_grads = (
        wide / (jnp.sqrt(0.999 * second_moment[None, :] + 0.001 * wide * wide) + 1e-08)
    ).astype(jnp.bfloat16)
    rows_all = jnp.concatenate([adam_grads, val_grads], axis=0)
    height = rows_all.shape[0]

    def one_block(position, summed):
        segment = lax.dynamic_slice_in_dim(rows_all, position * PB, PB, 1)
        matches = (slot_blocks == first_block + position).astype(jnp.int32)
        seeds_now = jnp.sum(slot_seeds * matches, axis=1)
        matrices = (jax.vmap(signs_for)(seeds_now) * factor).astype(jnp.bfloat16)
        partial_out = jnp.einsum(
            "rp,kpf->rkf", segment, matrices, preferred_element_type=jnp.float32
        )
        placing = matches.astype(jnp.float32).reshape(SLOTS, groups, per_group)
        return summed + jnp.einsum(
            "rkf,kgh->grhf", partial_out, placing, precision=lax.Precision.HIGHEST
        )

    start_sum = jnp.zeros((groups, height, per_group, FB), jnp.float32)
    summed = lax.fori_loop(0, local_blocks, one_block, start_sum)
    mine = lax.psum_scatter(
        summed.reshape(groups, height, 128), "feat", scatter_dimension=0, tiled=True
    )
    cand_part = mine[:, :ncand, :]
    val_part = mine[:, ncand:, :]
    cand_sq, val_sq = lax.psum((squares(cand_part), squares(val_part)), "feat")
    val_unit = val_part / jnp.sqrt(val_sq + 1e-06)[None, :, None]
    val_all = lax.all_gather(val_unit, "cand", axis=1, tiled=True)
    dots = jnp.einsum("gih,gvh->iv", cand_part, val_all, precision=lax.Precision.HIGHEST)
    tile = jnp.sum(dots.reshape(ncand, -1, VPT), axis=2) / VPT
    total = lax.psum(tile, "feat")
    width_own = total.shape[1] // lax.axis_size("feat")
    owned = lax.dynamic_slice_in_dim(total, lax.axis_index("feat") * width_own, width_own, 1)
    cand_norm = jnp.sqrt(cand_sq + 1e-06)
    return owned / cand_norm[:, None]


def solution(mesh):
    placed = (P("cand", "feat"), P("cand", "feat"), P("feat"), P(), P())
    return jax.shard_map(
        body, mesh=mesh, in_specs=placed, out_specs=P("cand", "feat"), check_vma=False
    )
```

profile of v0, /device:TPU:0, one launch (start us, length us, event | category | flops | bytes accessed | tf_op | source)
XLA Modules:
  0.0 388.0 jit_solution(3409171600617798099)
XLA Ops:
  6.5 0.0 copy-start
  6.5 0.0 reduce-scatter.2.cloned.1.call-start
  6.5 1.1 broadcast_multiply_fusion
  7.7 0.8 copy.16
  8.5 0.8 copy.17
  9.2 9.5 %fusion.14 = bf16[64,65536]{1,0:T(8,128)(2,1)S(1)} fusion(bf16[64,65536]{1,0:T(8,128)(2,1)} %param.7, f32[65536]{0:T(1024)S(1)} %broadcast_multiply_fusion), kind=kLoop, calls=%fused_computation.25 | loop fusion | flops 29360128 | bytes 17039360 | tf_op jit(solution)/shard_map/convert_element_type | solution.py:43
  18.8 0.0 copy-done
  18.8 6.3 %pad_maximum_fusion = bf16[80,65536]{1,0:T(8,128)(2,1)} fusion(bf16[16,65536]{1,0:T(8,128)(2,1)S(1)} %copy-done, bf16[64,65536]{1,0:T(8,128)(2,1)S(1)} %fusion.14), kind=kLoop, calls=%fused_computation.29 | loop fusion | flops 20971520 | bytes 20971520 | tf_op jit(solution)/shard_map/concatenate | solution.py:44
  25.1 148.3 %while.16 = (s32[]{:T(128)}, f32[64,80,2,64]{1,0,3,2:T(8,128)}, s32[]{:T(128)}, s32[8,128]{0,1:T(8,128)S(1)}, bf16[80,65536]{1,0:T(8,128)(2,1)}, /*index=5*/s32[...) while((s32[]{:T(128)}, f32[64,80,2,64]{1,0,3,2:T(8,128)}, s32[]{:T(128)}, ...), condition=%wide.region_2.0_spmd.clone, body=%wide.region_0.0_spmd.clone.sunk | while | flops 802436160 | bytes 23841520 | solution.py:61
  25.2 8.3 %fusion.32 = bf16[8,8192,64]{1,2,0:T(8,128)(2,1)S(1)} fusion(s32[64]{0:T(128)S(1)} %iota_multiply_fusion.4, s32[8192]{0:T(1024)S(1)} %iota_multiply_fusion.5, s32[8]{0:T(128)S(1)} %select_reduce_fusion.2), kind=kLoop, calls=%fused_computation.10.clone.1 | loop fusion | flops 67108864 | bytes 8421664 | tf_op jit(solution)/shard_map/while/body/eval_jaxpr/convert_element_type | solution.py:51
  33.5 3.7 fusion.33
  37.2 5.1 %bitcast_add_fusion.2 = f32[64,80,2,64]{1,0,3,2:T(8,128)} fusion(f32[64,80,2,64]{1,0,3,2:T(8,128)} %get-tuple-element.261, pred[]{:T(512)S(6)} %compare.3, f32[80,8,64]{0,2,1:T(8,128)S(1)} %bitcast.32, f32[8,64,2,1]{0,2,1,3:T(2,128)S(1)} %bitcast.33), kind=kOutput, calls=%fused_computation.11.clone.1 | convolution fusion | flops 64225280 | bytes 5410817 | tf_op jit(solution)/shard_map/while/body/eval_jaxpr/rkf,kgh->grhf/dot_general | solution.py:56
  42.3 8.3 %fusion.32 = bf16[8,8192,64]{1,2,0:T(8,128)(2,1)S(1)} fusion(s32[64]{0:T(128)S(1)} %iota_multiply_fusion.4, s32[8192]{0:T(1024)S(1)} %iota_multiply_fusion.5, s32[8]{0:T(128)S(1)} %select_reduce_fusion.2), kind=kLoop, calls=%fused_computation.10.clone.1 | loop fusion | flops 67108864 | bytes 8421664 | tf_op jit(solution)/shard_map/while/body/eval_jaxpr/convert_element_type | solution.py:51
  50.7 3.7 fusion.33
  54.4 6.6 %bitcast_add_fusion.2 = f32[64,80,2,64]{1,0,3,2:T(8,128)} fusion(f32[64,80,2,64]{1,0,3,2:T(8,128)} %get-tuple-element.261, pred[]{:T(512)S(6)} %compare.3, f32[80,8,64]{0,2,1:T(8,128)S(1)} %bitcast.32, f32[8,64,2,1]{0,2,1,3:T(2,128)S(1)} %bitcast.33), kind=kOutput, calls=%fused_computation.11.clone.1 | convolution fusion | flops 64225280 | bytes 5410817 | tf_op jit(solution)/shard_map/while/body/eval_jaxpr/rkf,kgh->grhf/dot_general | solution.py:56
  61.1 8.3 %fusion.32 = bf16[8,8192,64]{1,2,0:T(8,128)(2,1)S(1)} fusion(s32[64]{0:T(128)S(1)} %iota_multiply_fusion.4, s32[8192]{0:T(1024)S(1)} %iota_multiply_fusion.5, s32[8]{0:T(128)S(1)} %select_reduce_fusion.2), kind=kLoop, calls=%fused_computation.10.clone.1 | loop fusion | flops 67108864 | bytes 8421664 | tf_op jit(solution)/shard_map/while/body/eval_jaxpr/convert_element_type | solution.py:51
  69.4 3.7 fusion.33
  73.1 6.6 %bitcast_add_fusion.2 = f32[64,80,2,64]{1,0,3,2:T(8,128)} fusion(f32[64,80,2,64]{1,0,3,2:T(8,128)} %get-tuple-element.261, pred[]{:T(512)S(6)} %compare.3, f32[80,8,64]{0,2,1:T(8,128)S(1)} %bitcast.32, f32[8,64,2,1]{0,2,1,3:T(2,128)S(1)} %bitcast.33), kind=kOutput, calls=%fused_computation.11.clone.1 | convolution fusion | flops 64225280 | bytes 5410817 | tf_op jit(solution)/shard_map/while/body/eval_jaxpr/rkf,kgh->grhf/dot_general | solution.py:56
  79.8 8.3 %fusion.32 = bf16[8,8192,64]{1,2,0:T(8,128)(2,1)S(1)} fusion(s32[64]{0:T(128)S(1)} %iota_multiply_fusion.4, s32[8192]{0:T(1024)S(1)} %iota_multiply_fusion.5, s32[8]{0:T(128)S(1)} %select_reduce_fusion.2), kind=kLoop, calls=%fused_computation.10.clone.1 | loop fusion | flops 67108864 | bytes 8421664 | tf_op jit(solution)/shard_map/while/body/eval_jaxpr/convert_element_type | solution.py:51
  88.1 3.7 fusion.33
  91.8 6.6 %bitcast_add_fusion.2 = f32[64,80,2,64]{1,0,3,2:T(8,128)} fusion(f32[64,80,2,64]{1,0,3,2:T(8,128)} %get-tuple-element.261, pred[]{:T(512)S(6)} %compare.3, f32[80,8,64]{0,2,1:T(8,128)S(1)} %bitcast.32, f32[8,64,2,1]{0,2,1,3:T(2,128)S(1)} %bitcast.33), kind=kOutput, calls=%fused_computation.11.clone.1 | convolution fusion | flops 64225280 | bytes 5410817 | tf_op jit(solution)/shard_map/while/body/eval_jaxpr/rkf,kgh->grhf/dot_general | solution.py:56
  98.5 8.3 %fusion.32 = bf16[8,8192,64]{1,2,0:T(8,128)(2,1)S(1)} fusion(s32[64]{0:T(128)S(1)} %iota_multiply_fusion.4, s32[8192]{0:T(1024)S(1)} %iota_multiply_fusion.5, s32[8]{0:T(128)S(1)} %select_reduce_fusion.2), kind=kLoop, calls=%fused_computation.10.clone.1 | loop fusion | flops 67108864 | bytes 8421664 | tf_op jit(solution)/shard_map/while/body/eval_jaxpr/convert_element_type | solution.py:51
  106.9 3.7 fusion.33
  110.6 6.6 %bitcast_add_fusion.2 = f32[64,80,2,64]{1,0,3,2:T(8,128)} fusion(f32[64,80,2,64]{1,0,3,2:T(8,128)} %get-tuple-element.261, pred[]{:T(512)S(6)} %compare.3, f32[80,8,64]{0,2,1:T(8,128)S(1)} %bitcast.32, f32[8,64,2,1]{0,2,1,3:T(2,128)S(1)} %bitcast.33), kind=kOutput, calls=%fused_computation.11.clone.1 | convolution fusion | flops 64225280 | bytes 5410817 | tf_op jit(solution)/shard_map/while/body/eval_jaxpr/rkf,kgh->grhf/dot_general | solution.py:56
  117.3 8.3 %fusion.32 = bf16[8,8192,64]{1,2,0:T(8,128)(2,1)S(1)} fusion(s32[64]{0:T(128)S(1)} %iota_multiply_fusion.4, s32[8192]{0:T(1024)S(1)} %iota_multiply_fusion.5, s32[8]{0:T(128)S(1)} %select_reduce_fusion.2), kind=kLoop, calls=%fused_computation.10.clone.1 | loop fusion | flops 67108864 | bytes 8421664 | tf_op jit(solution)/shard_map/while/body/eval_jaxpr/convert_element_type | solution.py:51
  125.6 3.7 fusion.33
  129.3 6.6 %bitcast_add_fusion.2 = f32[64,80,2,64]{1,0,3,2:T(8,128)} fusion(f32[64,80,2,64]{1,0,3,2:T(8,128)} %get-tuple-element.261, pred[]{:T(512)S(6)} %compare.3, f32[80,8,64]{0,2,1:T(8,128)S(1)} %bitcast.32, f32[8,64,2,1]{0,2,1,3:T(2,128)S(1)} %bitcast.33), kind=kOutput, calls=%fused_computation.11.clone.1 | convolution fusion | flops 64225280 | bytes 5410817 | tf_op jit(solution)/shard_map/while/body/eval_jaxpr/rkf,kgh->grhf/dot_general | solution.py:56
  136.0 8.3 %fusion.32 = bf16[8,8192,64]{1,2,0:T(8,128)(2,1)S(1)} fusion(s32[64]{0:T(128)S(1)} %iota_multiply_fusion.4, s32[8192]{0:T(1024)S(1)} %iota_multiply_fusion.5, s32[8]{0:T(128)S(1)} %select_reduce_fusion.2), kind=kLoop, calls=%fused_computation.10.clone.1 | loop fusion | flops 67108864 | bytes 8421664 | tf_op jit(solution)/shard_map/while/body/eval_jaxpr/convert_element_type | solution.py:51
  144.3 3.7 fusion.33
  148.0 6.6 %bitcast_add_fusion.2 = f32[64,80,2,64]{1,0,3,2:T(8,128)} fusion(f32[64,80,2,64]{1,0,3,2:T(8,128)} %get-tuple-element.261, pred[]{:T(512)S(6)} %compare.3, f32[80,8,64]{0,2,1:T(8,128)S(1)} %bitcast.32, f32[8,64,2,1]{0,2,1,3:T(2,128)S(1)} %bitcast.33), kind=kOutput, calls=%fused_computation.11.clone.1 | convolution fusion | flops 64225280 | bytes 5410817 | tf_op jit(solution)/shard_map/while/body/eval_jaxpr/rkf,kgh->grhf/dot_general | solution.py:56
  154.7 8.3 %fusion.32 = bf16[8,8192,64]{1,2,0:T(8,128)(2,1)S(1)} fusion(s32[64]{0:T(128)S(1)} %iota_multiply_fusion.4, s32[8192]{0:T(1024)S(1)} %iota_multiply_fusion.5, s32[8]{0:T(128)S(1)} %select_reduce_fusion.2), kind=kLoop, calls=%fused_computation.10.clone.1 | loop fusion | flops 67108864 | bytes 8421664 | tf_op jit(solution)/shard_map/while/body/eval_jaxpr/convert_element_type | solution.py:51
  163.1 3.7 fusion.33
  166.8 6.6 %bitcast_add_fusion.2 = f32[64,80,2,64]{1,0,3,2:T(8,128)} fusion(f32[64,80,2,64]{1,0,3,2:T(8,128)} %get-tuple-element.261, pred[]{:T(512)S(6)} %compare.3, f32[80,8,64]{0,2,1:T(8,128)S(1)} %bitcast.32, f32[8,64,2,1]{0,2,1,3:T(2,128)S(1)} %bitcast.33), kind=kOutput, calls=%fused_computation.11.clone.1 | convolution fusion | flops 64225280 | bytes 5410817 | tf_op jit(solution)/shard_map/while/body/eval_jaxpr/rkf,kgh->grhf/dot_general | solution.py:56
  173.4 5.2 %copy.19 = f32[64,80,128]{2,1,0:T(8,128)} copy(f32[64,80,128]{1,0,2:T(8,128)} %bitcast.31) | data formatting | bytes 5242880 | tf_op jit(solution)/shard_map/reshape | solution.py:63
  178.6 0.0 reduce-scatter.2.cloned.1.call-update
  178.6 79.4 %reduce-scatter.2.cloned.1.call-done = f32[4,80,128]{2,1,0:T(8,128)} async-done(((f32[64,80,128]{2,1,0:T(8,128)}), f32[4,80,128]{2,1,0:T(8,128)}) %reduce-scatter.2.cloned.1.call-update) | async-done | bytes 163856 | tf_op jit(solution)/shard_map/reduce_scatter | solution.py:62
  258.0 0.9 multiply_reduce_fusion.1
  258.9 32.8 %psum.21 = f32[16]{0:T(128)S(1)} all-reduce(f32[16]{0:T(128)S(1)} %multiply_reduce_fusion.1), channel_id=1, replica_groups=mesh['feat'=16,'cand'=16] {'feat'}, use_global_device_ids=true, to_apply=%region_5.0 | all-reduce | flops 16 | bytes 128 | tf_op jit(solution)/shard_map/psum | solution.py:67
  291.7 0.8 slice_divide_fusion
  292.5 25.5 %all_gather.3 = f32[4,256,128]{2,1,0:T(8,128)S(1)} all-gather(f32[4,16,128]{2,1,0:T(8,128)S(1)} %slice_divide_fusion), channel_id=1, replica_groups=mesh['feat'=16,'cand'=16] {'cand'}, dimensions={1}, use_global_device_ids=true | all-gather | bytes 557056 | tf_op jit(solution)/shard_map/all_gather | solution.py:69
  318.0 1.5 fusion.18
  319.5 0.1 reduce_sum.44
  319.6 1.0 multiply_reduce_fusion
  320.6 59.9 %all-reduce = (f32[64,64]{0,1:T(8,128)S(1)}, f32[64]{0:T(128)S(1)}) all-reduce(f32[64,64]{0,1:T(8,128)S(1)} %broadcast_multiply_fusion.1, f32[64]{0:T(128)S(1)} %multiply_reduce_fusion), channel_id=1, replica_groups=mesh['feat'=16,'cand'=16] {'feat'}, use_global_device_ids=true, to_apply=%region_7.0 | all-reduce | flops 4160 | bytes 33280 | tf_op jit(solution)/shard_map/psum | solution.py:72
  380.6 0.6 dynamic-slice_divide_fusion
  (36 shorter events, 0.5 us)
Async XLA Ops:
  6.5 12.2 %copy-start = (bf16[16,65536]{1,0:T(8,128)(2,1)S(1)}, bf16[16,65536]{1,0:T(8,128)(2,1)}, u32[]{:S(2)}) copy-start(bf16[16,65536]{1,0:T(8,128)(2,1)} %param.8) | copy-start | bytes 6291460
  6.5 251.5 %reduce-scatter.2.cloned.1.call-start = ((), (), s32[]{:S(2)}) async-start(), calls=%async_computation.1 | async-start | bytes 2785280 | tf_op jit(solution)/shard_map/reduce_scatter | solution.py:62
Sparse Core Ops, SparseCore 0:
  178.7 79.2 reduce-scatter.1
where the time goes:
time: 389 us; the launch traced here: 388 us
  blocking collectives  118 us (30%)
  other arithmetic  87.5 us (22%)
  matrix products  82.5 us (21%)
  waiting for transfers between devices  79.4 us (20%)
  between operations  13.4 us (3%)
  local copies, waits for them, and re-layouts  6.73 us (2%)
    reduce_scatter x1, waiting for transfers between devices, body(): lax.psum_scatter(summed.reshape(groups, height, 128), 'feat', scatter_dim...  79.4 us
    convert_element_type x8, other arithmetic, one_block(): matrices = (jax.vmap(signs_for)(seeds_now) * factor).astype(jnp.bfloat16)  66.6 us
    psum x1, blocking collectives, body(): total = lax.psum(tile, 'feat')  59.9 us
    dot_general x8, matrix products, one_block(): jnp.einsum('rkf,kgh->grhf', partial_out, placing, precision=lax.Precision...  51.4 us
    psum x1, blocking collectives, body(): cand_sq, val_sq = lax.psum((squares(cand_part), squares(val_part)), 'feat')  32.8 us
    while x8, matrix products  29.6 us
    all_gather x1, blocking collectives, body(): val_all = lax.all_gather(val_unit, 'cand', axis=1, tiled=True)  25.5 us
    convert_element_type x1, other arithmetic, body(): adam_grads = (wide / (jnp.sqrt(0.999 * second_moment[None, :] + 0.001 * w...  9.5 us
  transfers between devices with their start and end apart: 1, of which 1 were waited for; matrix products, arithmetic and copies ran while one was open for 0% of the time, Pallas kernels for 0%

commit v1 on v0

--- a/solution.py
+++ b/solution.py
@@ -69,7 +69,8 @@
     val_all = lax.all_gather(val_unit, "cand", axis=1, tiled=True)
     dots = jnp.einsum("gih,gvh->iv", cand_part, val_all, precision=lax.Precision.HIGHEST)
     tile = jnp.sum(dots.reshape(ncand, -1, VPT), axis=2) / VPT
-    total = lax.psum(tile, "feat")
+    parts = lax.all_gather(tile, "feat")
+    total = jnp.sum(parts, axis=0)
     width_own = total.shape[1] // lax.axis_size("feat")
     owned = lax.dynamic_slice_in_dim(total, lax.axis_index("feat") * width_own, width_own, 1)
     cand_norm = jnp.sqrt(cand_sq + 1e-06)

time: 389 us -> 364 us (0.936)
  blocking collectives: 118 us -> 90.8 us
    psum x1 -> x0, blocking collectives: 59.9 us -> none  [body(): total = lax.psum(tile, 'feat')]
    all_gather x0 -> x1, blocking collectives: none -> 32.4 us  [body(): parts = lax.all_gather(tile, 'feat')]
where the time goes in v1:
time: 364 us; the launch traced here: 361 us
  blocking collectives  90.8 us (25%)
  other arithmetic  87.5 us (24%)
  matrix products  82.5 us (23%)
  waiting for transfers between devices  79.4 us (22%)
  between operations  13.4 us (4%)
  local copies, waits for them, and re-layouts  6.96 us (2%)
    reduce_scatter x1, waiting for transfers between devices, body(): lax.psum_scatter(summed.reshape(groups, height, 128), 'feat', scatter_dim...  79.4 us
    convert_element_type x8, other arithmetic, one_block(): matrices = (jax.vmap(signs_for)(seeds_now) * factor).astype(jnp.bfloat16)  66.6 us
    dot_general x8, matrix products, one_block(): jnp.einsum('rkf,kgh->grhf', partial_out, placing, precision=lax.Precision...  51.4 us
    psum x1, blocking collectives, body(): cand_sq, val_sq = lax.psum((squares(cand_part), squares(val_part)), 'feat')  32.8 us
    all_gather x1, blocking collectives, body(): parts = lax.all_gather(tile, 'feat')  32.4 us
    while x8, matrix products  29.6 us
    all_gather x1, blocking collectives, body(): val_all = lax.all_gather(val_unit, 'cand', axis=1, tiled=True)  25.5 us
    convert_element_type x1, other arithmetic, body(): adam_grads = (wide / (jnp.sqrt(0.999 * second_moment[None, :] + 0.001 * w...  9.5 us
  transfers between devices with their start and end apart: 1, of which 1 were waited for; matrix products, arithmetic and copies ran while one was open for 0% of the time, Pallas kernels for 0%

profile of v1, /device:TPU:0, one launch (start us, length us, event | category | flops | bytes accessed | tf_op | source)
XLA Modules:
  0.0 360.8 jit_solution(15462680350430402034)
XLA Ops:
  6.5 0.0 copy-start
  6.5 0.0 reduce-scatter.2.cloned.1.call-start
  6.5 1.1 broadcast_multiply_fusion
  7.7 0.8 copy.40
  8.5 0.8 copy.41
  9.2 9.5 %fusion.14 = bf16[64,65536]{1,0:T(8,128)(2,1)S(1)} fusion(bf16[64,65536]{1,0:T(8,128)(2,1)} %param.7, f32[65536]{0:T(1024)S(1)} %broadcast_multiply_fusion), kind=kLoop, calls=%fused_computation.25 | loop fusion | flops 29360128 | bytes 17039360 | tf_op jit(solution)/shard_map/convert_element_type | solution.py:43
  18.8 0.0 copy-done
  18.8 6.3 %pad_maximum_fusion = bf16[80,65536]{1,0:T(8,128)(2,1)} fusion(bf16[16,65536]{1,0:T(8,128)(2,1)S(1)} %copy-done, bf16[64,65536]{1,0:T(8,128)(2,1)S(1)} %fusion.14), kind=kLoop, calls=%fused_computation.29 | loop fusion | flops 20971520 | bytes 20971520 | tf_op jit(solution)/shard_map/concatenate | solution.py:44
  25.1 148.3 %while.16 = (s32[]{:T(128)}, f32[64,80,2,64]{1,0,3,2:T(8,128)}, s32[]{:T(128)}, s32[8,128]{0,1:T(8,128)S(1)}, bf16[80,65536]{1,0:T(8,128)(2,1)}, /*index=5*/s32[...) while((s32[]{:T(128)}, f32[64,80,2,64]{1,0,3,2:T(8,128)}, s32[]{:T(128)}, ...), condition=%wide.region_2.0_spmd.clone, body=%wide.region_0.0_spmd.clone.sunk | while | flops 802436160 | bytes 23841520 | solution.py:61
  25.2 8.3 %fusion.32 = bf16[8,8192,64]{1,2,0:T(8,128)(2,1)S(1)} fusion(s32[64]{0:T(128)S(1)} %iota_multiply_fusion.4, s32[8192]{0:T(1024)S(1)} %iota_multiply_fusion.5, s32[8]{0:T(128)S(1)} %select_reduce_fusion.2), kind=kLoop, calls=%fused_computation.10.clone.1 | loop fusion | flops 67108864 | bytes 8421664 | tf_op jit(solution)/shard_map/while/body/eval_jaxpr/convert_element_type | solution.py:51
  33.5 3.7 %fusion.33 = f32[80,512]{0,1:S(1)} fusion(bf16[8192,512]{0,1:T(8,128)(2,1)S(1)} %bitcast.31, bf16[80,65536]{1,0:T(8,128)(2,1)} %get-tuple-element.292, s32[]{:T(128)S(6)} %select_n.16), kind=kOutput, calls=%fused_computation.12.clone.1 | convolution fusion | flops 671088640 | bytes 9961476 | tf_op jit(solution)/shard_map/while
  37.2 5.1 %bitcast_add_fusion.2 = f32[64,80,2,64]{1,0,3,2:T(8,128)} fusion(f32[64,80,2,64]{1,0,3,2:T(8,128)} %get-tuple-element.279, pred[]{:T(512)S(6)} %compare.3, f32[80,8,64]{0,2,1:T(8,128)S(1)} %bitcast.33, f32[8,64,2,1]{0,2,1,3:T(2,128)S(1)} %bitcast.34), kind=kOutput, calls=%fused_computation.11.clone.1 | convolution fusion | flops 64225280 | bytes 5410817 | tf_op jit(solution)/shard_map/while/body/eval_jaxpr/rkf,kgh->grhf/dot_general | solution.py:56
  42.3 8.3 %fusion.32 = bf16[8,8192,64]{1,2,0:T(8,128)(2,1)S(1)} fusion(s32[64]{0:T(128)S(1)} %iota_multiply_fusion.4, s32[8192]{0:T(1024)S(1)} %iota_multiply_fusion.5, s32[8]{0:T(128)S(1)} %select_reduce_fusion.2), kind=kLoop, calls=%fused_computation.10.clone.1 | loop fusion | flops 67108864 | bytes 8421664 | tf_op jit(solution)/shard_map/while/body/eval_jaxpr/convert_element_type | solution.py:51
  50.7 3.7 %fusion.33 = f32[80,512]{0,1:S(1)} fusion(bf16[8192,512]{0,1:T(8,128)(2,1)S(1)} %bitcast.31, bf16[80,65536]{1,0:T(8,128)(2,1)} %get-tuple-element.292, s32[]{:T(128)S(6)} %select_n.16), kind=kOutput, calls=%fused_computation.12.clone.1 | convolution fusion | flops 671088640 | bytes 9961476 | tf_op jit(solution)/shard_map/while
  54.4 6.6 %bitcast_add_fusion.2 = f32[64,80,2,64]{1,0,3,2:T(8,128)} fusion(f32[64,80,2,64]{1,0,3,2:T(8,128)} %get-tuple-element.279, pred[]{:T(512)S(6)} %compare.3, f32[80,8,64]{0,2,1:T(8,128)S(1)} %bitcast.33, f32[8,64,2,1]{0,2,1,3:T(2,128)S(1)} %bitcast.34), kind=kOutput, calls=%fused_computation.11.clone.1 | convolution fusion | flops 64225280 | bytes 5410817 | tf_op jit(solution)/shard_map/while/body/eval_jaxpr/rkf,kgh->grhf/dot_general | solution.py:56
  61.1 8.3 %fusion.32 = bf16[8,8192,64]{1,2,0:T(8,128)(2,1)S(1)} fusion(s32[64]{0:T(128)S(1)} %iota_multiply_fusion.4, s32[8192]{0:T(1024)S(1)} %iota_multiply_fusion.5, s32[8]{0:T(128)S(1)} %select_reduce_fusion.2), kind=kLoop, calls=%fused_computation.10.clone.1 | loop fusion | flops 67108864 | bytes 8421664 | tf_op jit(solution)/shard_map/while/body/eval_jaxpr/convert_element_type | solution.py:51
  69.4 3.7 %fusion.33 = f32[80,512]{0,1:S(1)} fusion(bf16[8192,512]{0,1:T(8,128)(2,1)S(1)} %bitcast.31, bf16[80,65536]{1,0:T(8,128)(2,1)} %get-tuple-element.292, s32[]{:T(128)S(6)} %select_n.16), kind=kOutput, calls=%fused_computation.12.clone.1 | convolution fusion | flops 671088640 | bytes 9961476 | tf_op jit(solution)/shard_map/while
  73.1 6.6 %bitcast_add_fusion.2 = f32[64,80,2,64]{1,0,3,2:T(8,128)} fusion(f32[64,80,2,64]{1,0,3,2:T(8,128)} %get-tuple-element.279, pred[]{:T(512)S(6)} %compare.3, f32[80,8,64]{0,2,1:T(8,128)S(1)} %bitcast.33, f32[8,64,2,1]{0,2,1,3:T(2,128)S(1)} %bitcast.34), kind=kOutput, calls=%fused_computation.11.clone.1 | convolution fusion | flops 64225280 | bytes 5410817 | tf_op jit(solution)/shard_map/while/body/eval_jaxpr/rkf,kgh->grhf/dot_general | solution.py:56
  79.8 8.3 %fusion.32 = bf16[8,8192,64]{1,2,0:T(8,128)(2,1)S(1)} fusion(s32[64]{0:T(128)S(1)} %iota_multiply_fusion.4, s32[8192]{0:T(1024)S(1)} %iota_multiply_fusion.5, s32[8]{0:T(128)S(1)} %select_reduce_fusion.2), kind=kLoop, calls=%fused_computation.10.clone.1 | loop fusion | flops 67108864 | bytes 8421664 | tf_op jit(solution)/shard_map/while/body/eval_jaxpr/convert_element_type | solution.py:51
  88.1 3.7 %fusion.33 = f32[80,512]{0,1:S(1)} fusion(bf16[8192,512]{0,1:T(8,128)(2,1)S(1)} %bitcast.31, bf16[80,65536]{1,0:T(8,128)(2,1)} %get-tuple-element.292, s32[]{:T(128)S(6)} %select_n.16), kind=kOutput, calls=%fused_computation.12.clone.1 | convolution fusion | flops 671088640 | bytes 9961476 | tf_op jit(solution)/shard_map/while
  91.8 6.6 %bitcast_add_fusion.2 = f32[64,80,2,64]{1,0,3,2:T(8,128)} fusion(f32[64,80,2,64]{1,0,3,2:T(8,128)} %get-tuple-element.279, pred[]{:T(512)S(6)} %compare.3, f32[80,8,64]{0,2,1:T(8,128)S(1)} %bitcast.33, f32[8,64,2,1]{0,2,1,3:T(2,128)S(1)} %bitcast.34), kind=kOutput, calls=%fused_computation.11.clone.1 | convolution fusion | flops 64225280 | bytes 5410817 | tf_op jit(solution)/shard_map/while/body/eval_jaxpr/rkf,kgh->grhf/dot_general | solution.py:56
  98.5 8.3 %fusion.32 = bf16[8,8192,64]{1,2,0:T(8,128)(2,1)S(1)} fusion(s32[64]{0:T(128)S(1)} %iota_multiply_fusion.4, s32[8192]{0:T(1024)S(1)} %iota_multiply_fusion.5, s32[8]{0:T(128)S(1)} %select_reduce_fusion.2), kind=kLoop, calls=%fused_computation.10.clone.1 | loop fusion | flops 67108864 | bytes 8421664 | tf_op jit(solution)/shard_map/while/body/eval_jaxpr/convert_element_type | solution.py:51
  106.9 3.7 %fusion.33 = f32[80,512]{0,1:S(1)} fusion(bf16[8192,512]{0,1:T(8,128)(2,1)S(1)} %bitcast.31, bf16[80,65536]{1,0:T(8,128)(2,1)} %get-tuple-element.292, s32[]{:T(128)S(6)} %select_n.16), kind=kOutput, calls=%fused_computation.12.clone.1 | convolution fusion | flops 671088640 | bytes 9961476 | tf_op jit(solution)/shard_map/while
  110.6 6.6 %bitcast_add_fusion.2 = f32[64,80,2,64]{1,0,3,2:T(8,128)} fusion(f32[64,80,2,64]{1,0,3,2:T(8,128)} %get-tuple-element.279, pred[]{:T(512)S(6)} %compare.3, f32[80,8,64]{0,2,1:T(8,128)S(1)} %bitcast.33, f32[8,64,2,1]{0,2,1,3:T(2,128)S(1)} %bitcast.34), kind=kOutput, calls=%fused_computation.11.clone.1 | convolution fusion | flops 64225280 | bytes 5410817 | tf_op jit(solution)/shard_map/while/body/eval_jaxpr/rkf,kgh->grhf/dot_general | solution.py:56
  117.3 8.3 %fusion.32 = bf16[8,8192,64]{1,2,0:T(8,128)(2,1)S(1)} fusion(s32[64]{0:T(128)S(1)} %iota_multiply_fusion.4, s32[8192]{0:T(1024)S(1)} %iota_multiply_fusion.5, s32[8]{0:T(128)S(1)} %select_reduce_fusion.2), kind=kLoop, calls=%fused_computation.10.clone.1 | loop fusion | flops 67108864 | bytes 8421664 | tf_op jit(solution)/shard_map/while/body/eval_jaxpr/convert_element_type | solution.py:51
  125.6 3.7 %fusion.33 = f32[80,512]{0,1:S(1)} fusion(bf16[8192,512]{0,1:T(8,128)(2,1)S(1)} %bitcast.31, bf16[80,65536]{1,0:T(8,128)(2,1)} %get-tuple-element.292, s32[]{:T(128)S(6)} %select_n.16), kind=kOutput, calls=%fused_computation.12.clone.1 | convolution fusion | flops 671088640 | bytes 9961476 | tf_op jit(solution)/shard_map/while
  129.3 6.6 %bitcast_add_fusion.2 = f32[64,80,2,64]{1,0,3,2:T(8,128)} fusion(f32[64,80,2,64]{1,0,3,2:T(8,128)} %get-tuple-element.279, pred[]{:T(512)S(6)} %compare.3, f32[80,8,64]{0,2,1:T(8,128)S(1)} %bitcast.33, f32[8,64,2,1]{0,2,1,3:T(2,128)S(1)} %bitcast.34), kind=kOutput, calls=%fused_computation.11.clone.1 | convolution fusion | flops 64225280 | bytes 5410817 | tf_op jit(solution)/shard_map/while/body/eval_jaxpr/rkf,kgh->grhf/dot_general | solution.py:56
  136.0 8.3 %fusion.32 = bf16[8,8192,64]{1,2,0:T(8,128)(2,1)S(1)} fusion(s32[64]{0:T(128)S(1)} %iota_multiply_fusion.4, s32[8192]{0:T(1024)S(1)} %iota_multiply_fusion.5, s32[8]{0:T(128)S(1)} %select_reduce_fusion.2), kind=kLoop, calls=%fused_computation.10.clone.1 | loop fusion | flops 67108864 | bytes 8421664 | tf_op jit(solution)/shard_map/while/body/eval_jaxpr/convert_element_type | solution.py:51
  144.3 3.7 %fusion.33 = f32[80,512]{0,1:S(1)} fusion(bf16[8192,512]{0,1:T(8,128)(2,1)S(1)} %bitcast.31, bf16[80,65536]{1,0:T(8,128)(2,1)} %get-tuple-element.292, s32[]{:T(128)S(6)} %select_n.16), kind=kOutput, calls=%fused_computation.12.clone.1 | convolution fusion | flops 671088640 | bytes 9961476 | tf_op jit(solution)/shard_map/while
  148.0 6.6 %bitcast_add_fusion.2 = f32[64,80,2,64]{1,0,3,2:T(8,128)} fusion(f32[64,80,2,64]{1,0,3,2:T(8,128)} %get-tuple-element.279, pred[]{:T(512)S(6)} %compare.3, f32[80,8,64]{0,2,1:T(8,128)S(1)} %bitcast.33, f32[8,64,2,1]{0,2,1,3:T(2,128)S(1)} %bitcast.34), kind=kOutput, calls=%fused_computation.11.clone.1 | convolution fusion | flops 64225280 | bytes 5410817 | tf_op jit(solution)/shard_map/while/body/eval_jaxpr/rkf,kgh->grhf/dot_general | solution.py:56
  154.7 8.3 %fusion.32 = bf16[8,8192,64]{1,2,0:T(8,128)(2,1)S(1)} fusion(s32[64]{0:T(128)S(1)} %iota_multiply_fusion.4, s32[8192]{0:T(1024)S(1)} %iota_multiply_fusion.5, s32[8]{0:T(128)S(1)} %select_reduce_fusion.2), kind=kLoop, calls=%fused_computation.10.clone.1 | loop fusion | flops 67108864 | bytes 8421664 | tf_op jit(solution)/shard_map/while/body/eval_jaxpr/convert_element_type | solution.py:51
  163.1 3.7 %fusion.33 = f32[80,512]{0,1:S(1)} fusion(bf16[8192,512]{0,1:T(8,128)(2,1)S(1)} %bitcast.31, bf16[80,65536]{1,0:T(8,128)(2,1)} %get-tuple-element.292, s32[]{:T(128)S(6)} %select_n.16), kind=kOutput, calls=%fused_computation.12.clone.1 | convolution fusion | flops 671088640 | bytes 9961476 | tf_op jit(solution)/shard_map/while
  166.8 6.6 %bitcast_add_fusion.2 = f32[64,80,2,64]{1,0,3,2:T(8,128)} fusion(f32[64,80,2,64]{1,0,3,2:T(8,128)} %get-tuple-element.279, pred[]{:T(512)S(6)} %compare.3, f32[80,8,64]{0,2,1:T(8,128)S(1)} %bitcast.33, f32[8,64,2,1]{0,2,1,3:T(2,128)S(1)} %bitcast.34), kind=kOutput, calls=%fused_computation.11.clone.1 | convolution fusion | flops 64225280 | bytes 5410817 | tf_op jit(solution)/shard_map/while/body/eval_jaxpr/rkf,kgh->grhf/dot_general | solution.py:56
  173.4 5.2 %copy.43 = f32[64,80,128]{2,1,0:T(8,128)} copy(f32[64,80,128]{1,0,2:T(8,128)} %bitcast.32) | data formatting | bytes 5242880 | tf_op jit(solution)/shard_map/reshape | solution.py:63
  178.6 0.0 reduce-scatter.2.cloned.1.call-update
  178.6 79.4 %reduce-scatter.2.cloned.1.call-done = f32[4,80,128]{2,1,0:T(8,128)} async-done(((f32[64,80,128]{2,1,0:T(8,128)}), f32[4,80,128]{2,1,0:T(8,128)}) %reduce-scatter.2.cloned.1.call-update) | async-done | bytes 163856 | tf_op jit(solution)/shard_map/reduce_scatter | solution.py:62
  258.0 1.0 multiply_reduce_fusion
  259.0 0.9 multiply_reduce_fusion.1
  259.9 32.8 %all-reduce = (f32[16]{0:T(128)S(1)}, f32[64]{0:T(128)S(1)}) all-reduce(f32[16]{0:T(128)S(1)} %multiply_reduce_fusion.1, f32[64]{0:T(128)S(1)} %multiply_reduce_fusion), channel_id=1, replica_groups=mesh['feat'=16,'cand'=16] {'feat'}, use_global_device_ids=true, to_apply=%region_5.0 | all-reduce | flops 80 | bytes 640 | tf_op jit(solution)/shard_map/psum | solution.py:67
  292.7 0.8 slice_divide_fusion
  293.5 25.5 %all_gather.7 = f32[4,256,128]{2,1,0:T(8,128)S(1)} all-gather(f32[4,16,128]{2,1,0:T(8,128)S(1)} %slice_divide_fusion), channel_id=1, replica_groups=mesh['feat'=16,'cand'=16] {'cand'}, dimensions={1}, use_global_device_ids=true | all-gather | bytes 557056 | tf_op jit(solution)/shard_map/all_gather | solution.py:69
  319.1 1.5 fusion.18
  320.5 0.1 reduce_sum.53
  320.6 0.1 copy.45
  320.7 32.4 %all-gather = f32[1024,64]{1,0:T(8,128)S(1)} all-gather(f32[64,64]{1,0:T(8,128)S(1)} %copy.45), channel_id=2, replica_groups=mesh['feat'=16,'cand'=16] {'feat'}, dimensions={0}, use_global_device_ids=true | all-gather | bytes 278528 | tf_op jit(solution)/shard_map/all_gather | solution.py:72
  353.2 0.1 constant_dynamic-slice_fusion
  353.3 0.1 copy.54
  353.4 0.6 broadcast_divide_fusion
  (37 shorter events, 0.6 us)
Async XLA Ops:
  6.5 12.2 %copy-start = (bf16[16,65536]{1,0:T(8,128)(2,1)S(1)}, bf16[16,65536]{1,0:T(8,128)(2,1)}, u32[]{:S(2)}) copy-start(bf16[16,65536]{1,0:T(8,128)(2,1)} %param.8) | copy-start | bytes 6291460
  6.5 251.5 %reduce-scatter.2.cloned.1.call-start = ((), (), s32[]{:S(2)}) async-start(), calls=%async_computation.1 | async-start | bytes 2785280 | tf_op jit(solution)/shard_map/reduce_scatter | solution.py:62
Sparse Core Ops, SparseCore 0:
  178.7 79.2 reduce-scatter.1
